TPU v7x, 512 devices: a whole 4x4x16 slice. The times are simulated.
512 devices in a mesh: dp: 4 (over y), expert: 32 (over z, core), tensor: 4 (over x).
Axes of the slice: x: 4, y: 4, z: 16, core: 2. Of those that a mesh axis runs over, the one named last changes fastest.
Arguments:
- tokens: bfloat16 [16384, 2048], P(('dp', 'expert')), may hold values from -6 to 6
- cotangent: bfloat16 [16384, 2048], P(('dp', 'expert')), may hold values from -6 to 6
- expert_ids: int32 [16384, 1], P(('dp', 'expert')), may hold values from 0 to 31; in each aligned block of 128 rows (0 to 127, 128 to 255, ...) at most 8 rows name the same one
- gate_weight: bfloat16 [32, 2048, 1408], P('expert', 'dp', 'tensor'), may hold values from -0.125 to 0.125
- up_weight: bfloat16 [32, 2048, 1408], P('expert', 'dp', 'tensor'), may hold values from -0.125 to 0.125
- down_weight: bfloat16 [32, 2048, 1408], P('expert', 'dp', 'tensor'), may hold values from -0.15625 to 0.15625
Outputs:
- grad_tokens: bfloat16 [16384, 2048], P(('dp', 'expert'), 'tensor')
- grad_gate: bfloat16 [32, 2048, 1408], P('expert', 'dp', 'tensor')
- grad_up: bfloat16 [32, 2048, 1408], P('expert', 'dp', 'tensor')
Inputs may be any that keep to these rules, and one draw needn't show every extreme that they name: `expert_ids`: among the 128 tokens of one block no expert id occurs more than 8 times, and in every draw some block holds some id exactly 8 times.
All inputs are finite; a program needn't handle non-finite values.
Results may differ from a plain program's by a relative error of at most 0.013.
Values may be sent and summed in bfloat16 or wider, within the bound.
A program may use at most 64 MiB of HBM per device.

v0:
```python
import jax
import jax.numpy as jnp
from jax import lax
from jax.sharding import PartitionSpec as P

CAP = 8


def bucket_matrix(expert_ids, expert_count, capacity):
    chosen = expert_ids[:, 0]
    columns = jnp.arange(expert_count, dtype=jnp.int32)
    onehot = (chosen[:, None] == columns[None, :]).astype(jnp.int32)
    earlier = jnp.cumsum(onehot, axis=0) - onehot
    position = jnp.sum(earlier * onehot, axis=1)
    target = chosen * capacity + position
    slot_rows = jnp.arange(expert_count * capacity, dtype=jnp.int32)
    return (slot_rows[:, None] == target[None, :]).astype(jnp.bfloat16)


def on_device(tokens, cotangent, expert_ids, gate_weight, up_weight, down_weight):
    owners = lax.axis_size("expert")
    shards = lax.axis_size("tensor")
    features = tokens.shape[1]
    part = features // shards
    local_experts = gate_weight.shape[0]
    expert_count = local_experts * owners
    slot_count = owners * CAP
    placer = bucket_matrix(expert_ids, expert_count, CAP)
    gate_full, down_full, up_full = (
        lax.all_gather(w, "dp", axis=1, tiled=True)[0]
        for w in (gate_weight, down_weight, up_weight)
    )
    start = lax.axis_index("tensor") * part
    mine = jnp.concatenate(
        [lax.dynamic_slice_in_dim(a, start, part, axis=1) for a in (tokens, cotangent)], axis=1
    )
    packed = jnp.dot(placer, mine, preferred_element_type=jnp.float32).astype(jnp.bfloat16)
    arrived = lax.all_to_all(
        packed.reshape(owners, CAP, 2 * part), "expert", split_axis=0, concat_axis=0, tiled=True
    ).reshape(slot_count, 2 * part)
    whole = lax.all_gather(arrived, "tensor", axis=0, tiled=False)
    inputs = jnp.concatenate([whole[t, :, :part] for t in range(shards)], axis=1)
    grads_in = jnp.concatenate([whole[t, :, part:] for t in range(shards)], axis=1)
    gate_act = jnp.dot(inputs, gate_full, preferred_element_type=jnp.float32)
    hidden_grad = jnp.dot(grads_in, down_full, preferred_element_type=jnp.float32)
    up_act = jnp.dot(inputs, up_full, preferred_element_type=jnp.float32)
    sigmoid_gate = jax.nn.sigmoid(gate_act)
    up_grad = (hidden_grad * gate_act * sigmoid_gate).astype(jnp.bfloat16)
    gate_grad = (
        hidden_grad * up_act * sigmoid_gate * (1.0 + gate_act * (1.0 - sigmoid_gate))
    ).astype(jnp.bfloat16)
    contract = (((1,), (1,)), ((), ()))
    partial_value = lax.dot_general(
        gate_grad, gate_full, contract, preferred_element_type=jnp.float32
    )
    partial_value = partial_value + lax.dot_general(
        up_grad, up_full, contract, preferred_element_type=jnp.float32
    )
    rows = (((0,), (0,)), ((), ()))
    gate_term = lax.dot_general(inputs, gate_grad, rows, preferred_element_type=jnp.float32)
    up_term = lax.dot_general(inputs, up_grad, rows, preferred_element_type=jnp.float32)
    summed = lax.psum_scatter(
        partial_value.astype(jnp.bfloat16), "tensor", scatter_dimension=1, tiled=True
    )
    grad_gate, grad_up = (
        lax.psum_scatter(term.astype(jnp.bfloat16), "dp", scatter_dimension=0, tiled=True)[None]
        for term in (gate_term, up_term)
    )
    returned = lax.all_to_all(
        summed.reshape(owners, CAP, part), "expert", split_axis=0, concat_axis=0, tiled=True
    ).reshape(slot_count, part)
    per_token = lax.dot_general(placer, returned, rows, preferred_element_type=jnp.float32)
    return (per_token.astype(jnp.bfloat16), grad_gate, grad_up)


def solution(mesh):
    placed = (
        P(("dp", "expert"), None),
        P(("dp", "expert"), None),
        P(("dp", "expert"), None),
        P("expert", "dp", "tensor"),
        P("expert", "dp", "tensor"),
        P("expert", "dp", "tensor"),
    )
    return jax.shard_map(
        on_device,
        mesh=mesh,
        in_specs=placed,
        out_specs=(
            P(("dp", "expert"), "tensor"),
            P("expert", "dp", "tensor"),
            P("expert", "dp", "tensor"),
        ),
        check_vma=False,
    )
```

profile of v0, /device:TPU:4, one launch (start us, length us, event | category | flops | bytes accessed | tf_op | source)
XLA Modules:
  0.0 313.7 jit_solution(8685269563842167810)
XLA Ops:
  7.2 0.0 all-gather.5.cloned.1.call-start
  7.2 0.7 fusion.36
  8.0 0.2 reduce_window_sum.11
  8.1 0.8 select_reduce_fusion
  9.0 0.7 multiply_add_fusion
  9.6 1.0 constant_dynamic-slice_fusion
  10.6 0.3 fusion.10
  10.9 49.1 %all_to_all.10 = bf16[32,8,1024]{2,1,0:T(8,128)(2,1)} all-to-all(bf16[32,8,1024]{2,1,0:T(8,128)(2,1)S(1)} %fusion.10), channel_id=1, replica_groups=mesh['dp'=4,'expert'=32,'tensor'=4] {'expert'}, dimensions={0} | all-to-all | bytes 1048576 | tf_op jit(solution)/shard_map/all_to_all | solution.py:38
  60.1 0.0 all-gather.5.cloned.1.call-update
  60.1 0.0 all-gather.11.cloned.1.call-start
  60.1 0.7 all-gather.11.cloned.1.call-update
  60.8 0.0 all-gather.7.cloned.1.call-start
  60.9 0.7 all-gather.7.cloned.1.call-update
  61.6 0.0 all-gather.9.cloned.1.call-start
  61.6 0.5 all-gather.9.cloned.1.call-update
  62.1 0.0 reduce-scatter.4.cloned.1.call-start
  62.2 26.8 %all-gather.5.cloned.1.call-done = bf16[4,256,1024]{2,1,0:T(8,128)(2,1)} async-done(((bf16[1,256,1024]{2,1,0:T(8,128)(2,1)}), bf16[4,256,1024]{2,1,0:T(8,128)(2,1)}) %all-gather.5.cloned.1.call-update) | async-done | bytes 2097168 | tf_op jit(solution)/shard_map/all_gather | solution.py:41
  89.0 1.7 slice_bitcast_fusion.3
  90.7 34.9 %all-gather.11.cloned.1.call-done = bf16[1,2048,352]{1,2,0:T(8,128)(2,1)} async-done(((bf16[1,512,352]{1,2,0:T(8,128)(2,1)}), bf16[1,2048,352]{1,2,0:T(8,128)(2,1)}) %all-gather.11.cloned.1.call-update) | async-done | bytes 1441808 | tf_op jit(solution)/shard_map/all_gather | solution.py:30
  125.6 1.9 fusion.3
  127.5 33.9 %all-gather.7.cloned.1.call-done = bf16[1,2048,352]{1,2,0:T(8,128)(2,1)} async-done(((bf16[1,512,352]{1,2,0:T(8,128)(2,1)}), bf16[1,2048,352]{1,2,0:T(8,128)(2,1)}) %all-gather.7.cloned.1.call-update) | async-done | bytes 1441808 | tf_op jit(solution)/shard_map/all_gather | solution.py:30
  161.5 1.9 multiply_convert_fusion
  163.4 33.8 %all-gather.9.cloned.1.call-done = bf16[1,2048,352]{1,2,0:T(8,128)(2,1)} async-done(((bf16[1,512,352]{1,2,0:T(8,128)(2,1)}), bf16[1,2048,352]{1,2,0:T(8,128)(2,1)}) %all-gather.9.cloned.1.call-update) | async-done | bytes 1441808 | tf_op jit(solution)/shard_map/all_gather | solution.py:30
  197.2 0.0 copy-start
  197.2 2.1 fusion.20
  199.3 0.0 copy-done
  199.3 0.0 copy-start.1
  199.3 0.7 fusion.1
  200.0 0.6 copy-done.1
  200.7 1.7 fusion
  202.4 0.0 reduce-scatter.4.cloned.1.call-update
  202.4 0.0 reduce-scatter.8.cloned.1.call-start
  202.4 1.6 convolution_convert_fusion
  204.1 0.0 reduce-scatter.8.cloned.1.call-update
  204.1 0.0 reduce-scatter.6.cloned.1.call-start
  204.2 1.7 convolution_convert_fusion.1
  205.8 0.0 reduce-scatter.6.cloned.1.call-update
  205.9 26.9 %reduce-scatter.4.cloned.1.call-done = bf16[256,512]{1,0:T(8,128)(2,1)} async-done(((bf16[256,2048]{1,0:T(8,128)(2,1)}), bf16[256,512]{1,0:T(8,128)(2,1)}) %reduce-scatter.4.cloned.1.call-update) | async-done | bytes 262160 | tf_op jit(solution)/shard_map/reduce_scatter | solution.py:62
  232.8 35.4 %all_to_all.11 = bf16[32,8,512]{2,1,0:T(8,128)(2,1)S(1)} all-to-all(bf16[32,8,512]{2,1,0:T(8,128)(2,1)} %bitcast.55), channel_id=1, replica_groups=mesh['dp'=4,'expert'=32,'tensor'=4] {'expert'}, dimensions={0} | all-to-all | bytes 524288 | tf_op jit(solution)/shard_map/all_to_all | solution.py:69
  268.2 0.9 convolution_convert_fusion.3
  269.0 1.5 reduce-scatter.8.cloned.1.call-done
  270.5 36.3 %reduce-scatter.6.cloned.1.call-done = bf16[512,352]{0,1:T(8,128)(2,1)} async-done(((bf16[2048,352]{0,1:T(8,128)(2,1)}), bf16[512,352]{0,1:T(8,128)(2,1)}) %reduce-scatter.6.cloned.1.call-update) | async-done | bytes 360464 | tf_op jit(solution)/shard_map/reduce_scatter | solution.py:66
Async XLA Ops:
  7.2 81.8 %all-gather.5.cloned.1.call-start = ((), (), s32[]{:S(2)}) async-start(), calls=%async_computation.5 | async-start | bytes 2621440 | tf_op jit(solution)/shard_map/all_gather | solution.py:41
  60.1 65.5 %all-gather.11.cloned.1.call-start = ((), (), s32[]{:S(2)}) async-start(), calls=%async_computation.8 | async-start | bytes 1802240 | tf_op jit(solution)/shard_map/all_gather | solution.py:30
  60.8 100.6 %all-gather.7.cloned.1.call-start = ((), (), s32[]{:S(2)}) async-start(), calls=%async_computation.6 | async-start | bytes 1802240 | tf_op jit(solution)/shard_map/all_gather | solution.py:30
  61.6 135.6 %all-gather.9.cloned.1.call-start = ((), (), s32[]{:S(2)}) async-start(), calls=%async_computation.7 | async-start | bytes 1802240 | tf_op jit(solution)/shard_map/all_gather | solution.py:30
  62.1 170.6 %reduce-scatter.4.cloned.1.call-start = ((), (), s32[]{:S(2)}) async-start(), calls=%async_computation.9 | async-start | bytes 1310720 | tf_op jit(solution)/shard_map/reduce_scatter | solution.py:62
  197.2 2.1 copy-start
  199.3 1.4 copy-start.1
  202.4 68.1 %reduce-scatter.8.cloned.1.call-start = ((), (), s32[]{:S(2)}) async-start(), calls=%async_computation.11 | async-start | bytes 1802240 | tf_op jit(solution)/shard_map/reduce_scatter | solution.py:66
  204.1 102.7 %reduce-scatter.6.cloned.1.call-start = ((), (), s32[]{:S(2)}) async-start(), calls=%async_computation.10 | async-start | bytes 1802240 | tf_op jit(solution)/shard_map/reduce_scatter | solution.py:66
Sparse Core Ops, SparseCore 0:
  60.2 28.7 all-gather.4
  91.1 34.4 all-gather.10
  127.7 33.7 all-gather.6
  163.4 33.7 all-gather.8
  202.5 30.1 reduce-scatter.3
  236.3 34.1 reduce-scatter.7
  274.2 32.5 reduce-scatter.5
where the time goes:
time: 314 us
  waiting for transfers between devices  196 us (62%)
  blocking collectives  84.6 us (27%)
  between operations  14.2 us (5%)
  matrix products  12.9 us (4%)
  local copies, waits for them, and re-layouts  3.33 us (1%)
    all_gather x3, waiting for transfers between devices, on_device(): lax.all_gather(w, 'dp', axis=1, tiled=True)[0]  103 us
    all_to_all x1, blocking collectives, on_device(): lax.all_to_all(packed.reshape(owners, CAP, 2 * part), 'expert', split_axi...  49.1 us
    reduce_scatter x2, waiting for transfers between devices, on_device(): lax.psum_scatter(term.astype(jnp.bfloat16), 'dp', scatter_dimension=0, ti...  37.8 us
    all_to_all x1, blocking collectives, on_device(): lax.all_to_all(summed.reshape(owners, CAP, part), 'expert', split_axis=0,...  35.4 us
    reduce_scatter x1, waiting for transfers between devices, on_device(): lax.psum_scatter(partial_value.astype(jnp.bfloat16), 'tensor', scatter_di...  26.9 us
    all_gather x1, waiting for transfers between devices, on_device(): whole = lax.all_gather(arrived, 'tensor', axis=0, tiled=False)  26.8 us
  transfers between devices with their start and end apart: 7, of which 7 were waited for; matrix products, arithmetic and copies ran while one was open for 3% of the time, Pallas kernels for 0%

commit v1 on v0

--- a/solution.py
+++ b/solution.py
@@ -4,6 +4,28 @@
 from jax.sharding import PartitionSpec as P
 
 CAP = 8
+
+
+def laid_out(blocks, dim):
+    lengths = list(blocks.shape[1:])
+    lengths[dim] *= blocks.shape[0]
+    return jnp.moveaxis(blocks, 0, dim).reshape(lengths)
+
+
+def collect(x, axis, dim):
+    count = lax.axis_size(axis)
+    pairs = [(i, (i + 1) % count) for i in range(count)]
+    back = [(b, a) for a, b in pairs]
+    lower, upper = ([], [])
+    for step in range(count - 1):
+        if step % 2 == 0:
+            lower.append(lax.ppermute(lower[-1] if lower else x, axis, pairs))
+        else:
+            upper.append(lax.ppermute(upper[-1] if upper else x, axis, back))
+    parts = jnp.stack([*lower[::-1], x, *upper])
+    shift = lax.axis_index(axis) - len(lower)
+    parts = parts[(jnp.arange(count) - shift) % count]
+    return laid_out(parts, dim)
 
 
 def bucket_matrix(expert_ids, expert_count, capacity):
@@ -27,8 +49,7 @@
     slot_count = owners * CAP
     placer = bucket_matrix(expert_ids, expert_count, CAP)
     gate_full, down_full, up_full = (
-        lax.all_gather(w, "dp", axis=1, tiled=True)[0]
-        for w in (gate_weight, down_weight, up_weight)
+        collect(w, "dp", 1)[0] for w in (gate_weight, down_weight, up_weight)
     )
     start = lax.axis_index("tensor") * part
     mine = jnp.concatenate(

time: 314 us -> 225 us (0.72)
  the two profiles are of different devices: /device:TPU:4 before, /device:TPU:2 now
where the time goes in v1:
time: 225 us; the launch traced here: 224 us
  blocking collectives  84.5 us (38%)
  waiting for transfers between devices  71.9 us (32%)
  starting transfers between devices  29.3 us (13%)
  between operations  14 us (6%)
  local copies, waits for them, and re-layouts  10.5 us (5%)
  matrix products  8.67 us (4%)
  other arithmetic  5.47 us (2%)
    all_to_all x1, blocking collectives, on_device(): lax.all_to_all(packed.reshape(owners, CAP, 2 * part), 'expert', split_axi...  49.1 us
    reduce_scatter x2, waiting for transfers between devices, on_device(): lax.psum_scatter(term.astype(jnp.bfloat16), 'dp', scatter_dimension=0, ti...  38.1 us
    all_to_all x1, blocking collectives, on_device(): lax.all_to_all(summed.reshape(owners, CAP, part), 'expert', split_axis=0,...  35.3 us
    ppermute x6, waiting for transfers between devices, collect(): lower.append(lax.ppermute(lower[-1] if lower else x, axis, pairs))  17.4 us
    reduce_scatter x1, waiting for transfers between devices, on_device(): lax.psum_scatter(partial_value.astype(jnp.bfloat16), 'tensor', scatter_di...  16.2 us
    ppermute x6, starting transfers between devices, collect(): lower.append(lax.ppermute(lower[-1] if lower else x, axis, pairs))  16.1 us
    ppermute x3, starting transfers between devices, collect(): upper.append(lax.ppermute(upper[-1] if upper else x, axis, back))  13.1 us
  transfers between devices with their start and end apart: 13, of which 9 were waited for; matrix products, arithmetic and copies ran while one was open for 6% of the time, Pallas kernels for 0%

profile of v1, /device:TPU:2, one launch (start us, length us, event | category | flops | bytes accessed | tf_op | source)
XLA Modules:
  0.0 224.3 jit_solution(12044603608505237441)
XLA Ops:
  7.2 0.0 all-gather.2.cloned.1.call-start
  7.2 0.7 fusion.19
  8.0 0.2 reduce_window_sum.11
  8.1 0.8 select_reduce_fusion
  9.0 0.7 multiply_add_fusion
  9.6 0.0 copy-start.3
  9.6 0.0 copy-start.4
  9.6 1.1 constant_dynamic-slice_fusion
  10.7 0.3 fusion.1
  11.0 49.1 %all_to_all.10 = bf16[32,8,1024]{2,1,0:T(8,128)(2,1)} all-to-all(bf16[32,8,1024]{2,1,0:T(8,128)(2,1)S(1)} %fusion.1), channel_id=1, replica_groups=mesh['dp'=4,'expert'=32,'tensor'=4] {'expert'}, dimensions={0} | all-to-all | bytes 1048576 | tf_op jit(solution)/shard_map/all_to_all | solution.py:59
  60.1 0.0 all-gather.2.cloned.1.call-update
  60.2 0.0 reduce-scatter.4.cloned.1.call-start
  60.2 0.0 copy-done.3
  60.2 3.5 %collective-permute-start.6 = (bf16[1,512,352]{1,2,0:T(8,128)(2,1)S(1)}, bf16[1,512,352]{1,2,0:T(8,128)(2,1)S(1)}, u32[]{:S(2)}, u32[]{:S(2)}) collective-permute-start(bf16[1,512,352]{1,2,0:T(8,128)(2,1)S(1)} %copy-done.3), channel_id=1, source_target_pairs={{0,128},{128,256},{256,384},{384,0},{1,129},{129,257},{257,385},{3... | collective-permute-start | bytes 1081352 | tf_op jit(solution)/shard_map/ppermute | solution.py:22
  63.7 0.0 copy-done.4
  63.7 3.5 %collective-permute-start = (bf16[1,512,352]{1,2,0:T(8,128)(2,1)S(1)}, bf16[1,512,352]{1,2,0:T(8,128)(2,1)}, u32[]{:S(2)}, u32[]{:S(2)}) collective-permute-start(bf16[1,512,352]{1,2,0:T(8,128)(2,1)S(1)} %copy-done.4), channel_id=1, source_target_pairs={{0,128},{128,256},{256,384},{384,0},{1,129},{129,257},{257,385},{3... | collective-permute-start | bytes 1081352 | tf_op jit(solution)/shard_map/ppermute | solution.py:22
  67.2 3.6 %collective-permute-start.8 = (bf16[1,512,352]{1,2,0:T(8,128)(2,1)S(1)}, bf16[1,512,352]{1,2,0:T(8,128)(2,1)S(1)}, u32[]{:S(2)}, u32[]{:S(2)}) collective-permute-start(bf16[1,512,352]{1,2,0:T(8,128)(2,1)S(1)} %copy-done.3), channel_id=1, source_target_pairs={{128,0},{256,128},{384,256},{0,384},{129,1},{257,129},{385,257},{1... | collective-permute-start | bytes 1081352 | tf_op jit(solution)/shard_map/ppermute | solution.py:24
  70.8 2.3 %collective-permute-start.3 = (bf16[1,512,352]{1,2,0:T(8,128)(2,1)}, bf16[1,512,352]{1,2,0:T(8,128)(2,1)}, u32[]{:S(2)}, u32[]{:S(2)}) collective-permute-start(bf16[1,512,352]{1,2,0:T(8,128)(2,1)} %param.10), channel_id=1, source_target_pairs={{0,128},{128,256},{256,384},{384,0},{1,129},{129,257},{257,385},{3... | collective-permute-start | bytes 1081352 | tf_op jit(solution)/shard_map/ppermute | solution.py:22
  73.1 1.5 collective-permute-done.6
  74.6 2.3 %collective-permute-start.7 = (bf16[1,512,352]{1,2,0:T(8,128)(2,1)S(1)}, bf16[1,512,352]{1,2,0:T(8,128)(2,1)S(1)}, u32[]{:S(2)}, u32[]{:S(2)}) collective-permute-start(bf16[1,512,352]{1,2,0:T(8,128)(2,1)S(1)} %collective-permute-done.6), channel_id=1, source_target_pairs={{0,128},{128,256},{256,384},{384,0},{1,129},{129,257},{257,385},{3... | collective-permute-start | bytes 1081352 | tf_op jit(solution)/shard_map/ppermute | solution.py:22
  76.9 4.8 %collective-permute-start.2 = (bf16[1,512,352]{1,2,0:T(8,128)(2,1)S(1)}, bf16[1,512,352]{1,2,0:T(8,128)(2,1)}, u32[]{:S(2)}, u32[]{:S(2)}) collective-permute-start(bf16[1,512,352]{1,2,0:T(8,128)(2,1)S(1)} %copy-done.4), channel_id=1, source_target_pairs={{128,0},{256,128},{384,256},{0,384},{129,1},{257,129},{385,257},{1... | collective-permute-start | bytes 1081352 | tf_op jit(solution)/shard_map/ppermute | solution.py:24
  81.6 0.8 collective-permute-done
  82.4 2.3 %collective-permute-start.1 = (bf16[1,512,352]{1,2,0:T(8,128)(2,1)}, bf16[1,512,352]{1,2,0:T(8,128)(2,1)}, u32[]{:S(2)}, u32[]{:S(2)}) collective-permute-start(bf16[1,512,352]{1,2,0:T(8,128)(2,1)} %collective-permute-done), channel_id=1, source_target_pairs={{0,128},{128,256},{256,384},{384,0},{1,129},{129,257},{257,385},{3... | collective-permute-start | bytes 1081352 | tf_op jit(solution)/shard_map/ppermute | solution.py:22
  84.7 0.0 collective-permute-done.8
  84.7 4.8 %collective-permute-start.5 = (bf16[1,512,352]{1,2,0:T(8,128)(2,1)}, bf16[1,512,352]{1,2,0:T(8,128)(2,1)}, u32[]{:S(2)}, u32[]{:S(2)}) collective-permute-start(bf16[1,512,352]{1,2,0:T(8,128)(2,1)} %param.10), channel_id=1, source_target_pairs={{128,0},{256,128},{384,256},{0,384},{129,1},{257,129},{385,257},{1... | collective-permute-start | bytes 1081352 | tf_op jit(solution)/shard_map/ppermute | solution.py:24
  89.5 0.6 collective-permute-done.3
  90.1 2.3 %collective-permute-start.4 = (bf16[1,512,352]{1,2,0:T(8,128)(2,1)}, bf16[1,512,352]{1,2,0:T(8,128)(2,1)}, u32[]{:S(2)}, u32[]{:S(2)}) collective-permute-start(bf16[1,512,352]{1,2,0:T(8,128)(2,1)} %collective-permute-done.3), channel_id=1, source_target_pairs={{0,128},{128,256},{256,384},{384,0},{1,129},{129,257},{257,385},{3... | collective-permute-start | bytes 1081352 | tf_op jit(solution)/shard_map/ppermute | solution.py:22
  92.4 5.3 %collective-permute-done.7 = bf16[1,512,352]{1,2,0:T(8,128)(2,1)S(1)} collective-permute-done((bf16[1,512,352]{1,2,0:T(8,128)(2,1)S(1)}, bf16[1,512,352]{1,2,0:T(8,128)(2,1)S(1)}, u32[]{:S(2)}, u32[]{:S(2)}) %collective-permute-start.7) | collective-permute-done | bytes 360480 | tf_op jit(solution)/shard_map/ppermute | solution.py:22
  97.8 0.2 maximum_bitcast_fusion.2
  97.9 0.6 gather_fusion.2
  98.6 1.3 copy.17
  99.9 0.0 collective-permute-done.2
  99.9 5.7 %collective-permute-done.1 = bf16[1,512,352]{1,2,0:T(8,128)(2,1)} collective-permute-done((bf16[1,512,352]{1,2,0:T(8,128)(2,1)}, bf16[1,512,352]{1,2,0:T(8,128)(2,1)}, u32[]{:S(2)}, u32[]{:S(2)}) %collective-permute-start.1) | collective-permute-done | bytes 360480 | tf_op jit(solution)/shard_map/ppermute | solution.py:22
  105.6 1.4 maximum_bitcast_fusion
  107.0 0.6 gather_fusion
  107.6 1.3 copy.15
  108.9 0.0 collective-permute-done.5
  108.9 3.5 %collective-permute-done.4 = bf16[1,512,352]{1,2,0:T(8,128)(2,1)} collective-permute-done((bf16[1,512,352]{1,2,0:T(8,128)(2,1)}, bf16[1,512,352]{1,2,0:T(8,128)(2,1)}, u32[]{:S(2)}, u32[]{:S(2)}) %collective-permute-start.4) | collective-permute-done | bytes 360480 | tf_op jit(solution)/shard_map/ppermute | solution.py:22
  112.5 1.5 maximum_bitcast_fusion.1
  113.9 0.6 gather_fusion.1
  114.6 1.4 copy.16
  115.9 0.0 all-gather.2.cloned.1.call-done
  116.0 1.7 slice_bitcast_fusion.3
  117.7 0.2 copy-done
  117.9 0.6 fusion.24
  118.5 0.8 copy-done.2
  119.3 0.0 copy-start.1
  119.3 0.6 multiply_convert_fusion
  119.9 0.8 copy-done.1
  120.7 0.6 fusion.4
  121.3 0.7 fusion.25
  122.0 1.7 fusion
  123.7 0.0 reduce-scatter.4.cloned.1.call-update
  123.7 0.0 reduce-scatter.8.cloned.1.call-start
  123.8 1.7 convolution_convert_fusion
  125.4 0.0 reduce-scatter.8.cloned.1.call-update
  125.5 0.0 reduce-scatter.6.cloned.1.call-start
  125.5 1.7 convolution_convert_fusion.1
  127.2 0.0 reduce-scatter.6.cloned.1.call-update
  127.2 16.2 %reduce-scatter.4.cloned.1.call-done = bf16[256,512]{1,0:T(8,128)(2,1)} async-done(((bf16[256,2048]{1,0:T(8,128)(2,1)}), bf16[256,512]{1,0:T(8,128)(2,1)}) %reduce-scatter.4.cloned.1.call-update) | async-done | bytes 262160 | tf_op jit(solution)/shard_map/reduce_scatter | solution.py:83
  143.4 35.3 %all_to_all.11 = bf16[32,8,512]{2,1,0:T(8,128)(2,1)S(1)} all-to-all(bf16[32,8,512]{2,1,0:T(8,128)(2,1)} %bitcast.76), channel_id=1, replica_groups=mesh['dp'=4,'expert'=32,'tensor'=4] {'expert'}, dimensions={0} | all-to-all | bytes 524288 | tf_op jit(solution)/shard_map/all_to_all | solution.py:90
  178.8 0.9 convolution_convert_fusion.3
  179.7 2.0 reduce-scatter.8.cloned.1.call-done
  181.7 36.1 %reduce-scatter.6.cloned.1.call-done = bf16[512,352]{0,1:T(8,128)(2,1)} async-done(((bf16[2048,352]{0,1:T(8,128)(2,1)}), bf16[512,352]{0,1:T(8,128)(2,1)}) %reduce-scatter.6.cloned.1.call-update) | async-done | bytes 360464 | tf_op jit(solution)/shard_map/reduce_scatter | solution.py:87
  (4 shorter events, 0.0 us)
Async XLA Ops:
  7.2 108.8 %all-gather.2.cloned.1.call-start = ((), (), s32[]{:S(2)}) async-start(), calls=%async_computation.5 | async-start | bytes 2621440 | tf_op jit(solution)/shard_map/all_gather | solution.py:62
  9.6 50.6 %copy-start.3 = (bf16[1,512,352]{1,2,0:T(8,128)(2,1)S(1)}, bf16[1,512,352]{1,2,0:T(8,128)(2,1)}, u32[]{:S(2)}) copy-start(bf16[1,512,352]{1,2,0:T(8,128)(2,1)} %param.9) | copy-start | bytes 1081348
  9.6 54.1 %copy-start.4 = (bf16[1,512,352]{1,2,0:T(8,128)(2,1)S(1)}, bf16[1,512,352]{1,2,0:T(8,128)(2,1)}, u32[]{:S(2)}) copy-start(bf16[1,512,352]{1,2,0:T(8,128)(2,1)} %param.11) | copy-start | bytes 1081348
  60.2 83.3 %reduce-scatter.4.cloned.1.call-start = ((), (), s32[]{:S(2)}) async-start(), calls=%async_computation.6 | async-start | bytes 1310720 | tf_op jit(solution)/shard_map/reduce_scatter | solution.py:83
  60.2 14.4 %collective-permute-start.6 = (bf16[1,512,352]{1,2,0:T(8,128)(2,1)S(1)}, bf16[1,512,352]{1,2,0:T(8,128)(2,1)S(1)}, u32[]{:S(2)}, u32[]{:S(2)}) collective-permute-start(bf16[1,512,352]{1,2,0:T(8,128)(2,1)S(1)} %copy-done.3), channel_id=1, source_target_pairs={{0,128},{128,256},{256,384},{384,0},{1,129},{129,257},{257,385},{3... | collective-permute-start | bytes 1081352 | tf_op jit(solution)/shard_map/ppermute | solution.py:22
  63.7 18.7 %collective-permute-start = (bf16[1,512,352]{1,2,0:T(8,128)(2,1)S(1)}, bf16[1,512,352]{1,2,0:T(8,128)(2,1)}, u32[]{:S(2)}, u32[]{:S(2)}) collective-permute-start(bf16[1,512,352]{1,2,0:T(8,128)(2,1)S(1)} %copy-done.4), channel_id=1, source_target_pairs={{0,128},{128,256},{256,384},{384,0},{1,129},{129,257},{257,385},{3... | collective-permute-start | bytes 1081352 | tf_op jit(solution)/shard_map/ppermute | solution.py:22
  67.2 17.5 %collective-permute-start.8 = (bf16[1,512,352]{1,2,0:T(8,128)(2,1)S(1)}, bf16[1,512,352]{1,2,0:T(8,128)(2,1)S(1)}, u32[]{:S(2)}, u32[]{:S(2)}) collective-permute-start(bf16[1,512,352]{1,2,0:T(8,128)(2,1)S(1)} %copy-done.3), channel_id=1, source_target_pairs={{128,0},{256,128},{384,256},{0,384},{129,1},{257,129},{385,257},{1... | collective-permute-start | bytes 1081352 | tf_op jit(solution)/shard_map/ppermute | solution.py:24
  70.8 19.4 %collective-permute-start.3 = (bf16[1,512,352]{1,2,0:T(8,128)(2,1)}, bf16[1,512,352]{1,2,0:T(8,128)(2,1)}, u32[]{:S(2)}, u32[]{:S(2)}) collective-permute-start(bf16[1,512,352]{1,2,0:T(8,128)(2,1)} %param.10), channel_id=1, source_target_pairs={{0,128},{128,256},{256,384},{384,0},{1,129},{129,257},{257,385},{3... | collective-permute-start | bytes 1081352 | tf_op jit(solution)/shard_map/ppermute | solution.py:22
  74.6 23.2 %collective-permute-start.7 = (bf16[1,512,352]{1,2,0:T(8,128)(2,1)S(1)}, bf16[1,512,352]{1,2,0:T(8,128)(2,1)S(1)}, u32[]{:S(2)}, u32[]{:S(2)}) collective-permute-start(bf16[1,512,352]{1,2,0:T(8,128)(2,1)S(1)} %collective-permute-done.6), channel_id=1, source_target_pairs={{0,128},{128,256},{256,384},{384,0},{1,129},{129,257},{257,385},{3... | collective-permute-start | bytes 1081352 | tf_op jit(solution)/shard_map/ppermute | solution.py:22
  76.9 23.0 %collective-permute-start.2 = (bf16[1,512,352]{1,2,0:T(8,128)(2,1)S(1)}, bf16[1,512,352]{1,2,0:T(8,128)(2,1)}, u32[]{:S(2)}, u32[]{:S(2)}) collective-permute-start(bf16[1,512,352]{1,2,0:T(8,128)(2,1)S(1)} %copy-done.4), channel_id=1, source_target_pairs={{128,0},{256,128},{384,256},{0,384},{129,1},{257,129},{385,257},{1... | collective-permute-start | bytes 1081352 | tf_op jit(solution)/shard_map/ppermute | solution.py:24
  82.4 23.2 %collective-permute-start.1 = (bf16[1,512,352]{1,2,0:T(8,128)(2,1)}, bf16[1,512,352]{1,2,0:T(8,128)(2,1)}, u32[]{:S(2)}, u32[]{:S(2)}) collective-permute-start(bf16[1,512,352]{1,2,0:T(8,128)(2,1)} %collective-permute-done), channel_id=1, source_target_pairs={{0,128},{128,256},{256,384},{384,0},{1,129},{129,257},{257,385},{3... | collective-permute-start | bytes 1081352 | tf_op jit(solution)/shard_map/ppermute | solution.py:22
  84.7 24.2 %collective-permute-start.5 = (bf16[1,512,352]{1,2,0:T(8,128)(2,1)}, bf16[1,512,352]{1,2,0:T(8,128)(2,1)}, u32[]{:S(2)}, u32[]{:S(2)}) collective-permute-start(bf16[1,512,352]{1,2,0:T(8,128)(2,1)} %param.10), channel_id=1, source_target_pairs={{128,0},{256,128},{384,256},{0,384},{129,1},{257,129},{385,257},{1... | collective-permute-start | bytes 1081352 | tf_op jit(solution)/shard_map/ppermute | solution.py:24
  90.1 22.3 %collective-permute-start.4 = (bf16[1,512,352]{1,2,0:T(8,128)(2,1)}, bf16[1,512,352]{1,2,0:T(8,128)(2,1)}, u32[]{:S(2)}, u32[]{:S(2)}) collective-permute-start(bf16[1,512,352]{1,2,0:T(8,128)(2,1)} %collective-permute-done.3), channel_id=1, source_target_pairs={{0,128},{128,256},{256,384},{384,0},{1,129},{129,257},{257,385},{3... | collective-permute-start | bytes 1081352 | tf_op jit(solution)/shard_map/ppermute | solution.py:22
  115.9 2.0 copy-start
  117.9 1.4 copy-start.2
  119.3 1.4 copy-start.1
  123.7 57.9 %reduce-scatter.8.cloned.1.call-start = ((), (), s32[]{:S(2)}) async-start(), calls=%async_computation.8 | async-start | bytes 1802240 | tf_op jit(solution)/shard_map/reduce_scatter | solution.py:87
  125.5 92.3 %reduce-scatter.6.cloned.1.call-start = ((), (), s32[]{:S(2)}) async-start(), calls=%async_computation.7 | async-start | bytes 1802240 | tf_op jit(solution)/shard_map/reduce_scatter | solution.py:87
Sparse Core Ops, SparseCore 0:
  60.3 29.0 all-gather.1
  123.9 19.5 reduce-scatter.3
  147.1 34.5 reduce-scatter.7
  185.2 32.5 reduce-scatter.5
